TPU v7x, 128 devices: a whole 4x4x4 slice. The times are simulated.
128 devices in a mesh: row: 16 (over x_lo, z, core), col: 8 (over x_hi, y).
Axes of the slice: x: 4 (x_hi: 2, x_lo: 2; x = x_hi * 2 + x_lo), y: 4, z: 4, core: 2. Of those that a mesh axis runs over, the one named last changes fastest.
Arguments:
- eigvecs: float32 [512, 262144], P(('row', 'col')), may hold values from -6 to 6
- panels: bfloat16 [8, 262144, 128], P('col', 'row'), may hold values from -0.01171875 to 0.01171875
- tfactors: bfloat16 [8, 128, 128], P('col'), as said below
- owners: int32 [4], replicated, may hold values from 0 to 7, as said below
- offsets: int32 [4], replicated, may hold values from 0 to 65408, as said below
Outputs:
- back: float32 [512, 262144], P('col', 'row')
Inputs may be any that keep to these rules, and one draw needn't show every extreme that they name: `owners`: distinct grid columns. `offsets`: multiples of 128. `tfactors`: each matrix is upper triangular with its diagonal between 1 and 8.
All inputs are finite; a program needn't handle non-finite values.
Results may differ from a plain program's by a relative error of at most 0.0003.
Values may be sent and summed in bfloat16 or wider, within the bound.
No kernel may reach another device: no remote copies, remote signals or barrier semaphores. Data moves between devices by JAX's collectives and lax.ppermute only.
A program may use at most 128 MiB of HBM per device.

v0:
```python
import jax
import jax.numpy as jnp
from jax import lax
from jax.sharding import PartitionSpec as P

PANELS = 4


def from_root(value, axis, root):
    mine = lax.axis_index(axis) == root
    return lax.psum(jnp.where(mine, value, jnp.zeros_like(value)), axis)


def reflector_block(stored, offset, first_row):
    row_ids = first_row + lax.broadcasted_iota(jnp.int32, stored.shape, 0)
    col_ids = lax.broadcasted_iota(jnp.int32, stored.shape, 1)
    below = row_ids - col_ids - offset
    unit = jnp.where(below == 0, jnp.float32(1.0), jnp.float32(0.0))
    return jnp.where(below > 0, stored.astype(jnp.float32), unit)


def local(eigvecs, panels, tfactors, owners, offsets):
    highest = lax.Precision.HIGHEST
    spread = lax.all_to_all(eigvecs, ("row", "col"), split_axis=1, concat_axis=0, tiled=True)
    field = lax.all_to_all(spread, "col", split_axis=0, concat_axis=1, tiled=True)
    local_rows = field.shape[1]
    first_row = lax.axis_index("row") * local_rows
    for panel in reversed(range(PANELS)):
        stored, triangle = (
            from_root(panels[0], "col", owners[panel]),
            from_root(tfactors[0], "col", owners[panel]),
        )
        reflector = reflector_block(stored, offsets[panel], first_row)
        partial_sum = jnp.dot(
            field, reflector, precision=highest, preferred_element_type=jnp.float32
        )
        projection = lax.psum(partial_sum, "row")
        coeffs = jnp.dot(
            projection,
            triangle.astype(jnp.float32).T,
            precision=highest,
            preferred_element_type=jnp.float32,
        )
        field = field - jnp.dot(
            coeffs, reflector.T, precision=highest, preferred_element_type=jnp.float32
        )
    return field


def solution(mesh):
    in_specs = (P(("row", "col"), None), P("col", "row", None), P("col", None, None), P(), P())
    out_specs = P("col", "row")
    return jax.shard_map(local, mesh=mesh, in_specs=in_specs, out_specs=out_specs, check_vma=False)
```

profile of v0, /device:TPU:0, one launch (start us, length us, event | category | flops | bytes accessed | tf_op | source)
XLA Modules:
  0.0 801.4 jit_solution(956062788617892617)
XLA Ops:
  6.5 0.0 all-reduce.7.cloned.1.call-start
  6.5 1.5 fusion.82
  10.5 7.4 select_bitcast_fusion
  18.0 0.0 all-reduce.7.cloned.1.call-update
  18.0 221.5 %all_to_all.35 = f32[4,128,2048]{2,0,1:T(4,128)} all-to-all(f32[4,128,2048]{2,0,1:T(4,128)} %bitcast.48), channel_id=1, replica_groups=mesh['row'=16,'col'=8] {'row','col'}, dimensions={1} | all-to-all | bytes 8388608 | tf_op jit(solution)/shard_map/all_to_all | solution.py:24
  239.5 5.3 all_to_all.29
  244.8 0.0 copy-start.3
  244.8 0.0 copy-start.4
  244.8 4.7 all-to-all-start.1
  249.5 0.0 all-reduce.5.cloned.1.call-start
  249.6 0.0 copy-done.3
  249.6 0.7 select_bitcast_fusion.4
  250.2 0.0 all-reduce.5.cloned.1.call-update
  250.3 0.0 copy-done.4
  250.3 0.7 fusion.81
  251.0 99.6 %all-to-all-done.1 = f32[8,64,2048]{2,1,0:T(8,128)} async-done(((f32[8,64,2048]{2,1,0:T(8,128)}), f32[8,64,2048]{2,1,0:T(8,128)}, u32[]{:S(2)}, u32[]{:S(2)}) %all-to-all-start.1) | async-done | bytes 4194336 | tf_op jit(solution)/shard_map/all_to_all | solution.py:25
  350.6 4.7 copy.8
  355.3 106.0 %all-reduce.7.cloned.1.call-done = (bf16[16384,128]{1,0:T(8,128)(2,1)}, bf16[16384,128]{1,0:T(8,128)(2,1)}, bf16[16384,128]{1,0:T(8,128)(2,1)}, bf16[16384,128]{1,0:T(8,128)(2,1)}) async-done(((bf16[16384,128]{1,0:T(8,128)(2,1)}, bf16[16384,128]{1,0:T(8,128)(2,1)}, bf16[16384,128]{1,0:T(8,128)(2,1)}, bf16[16384,128]{1,0:T(8,128)(2,1)}), (bf16[16384,128]{1,0:T(8,128)(2,1)}, bf16[16384,128]{1,0:T(8,128)(2,1)}, ...) | async-done | bytes 16777232 | tf_op jit(solution)/shard_map/psum | solution.py:11
  461.3 16.5 %fusion.56 = f32[64,128]{0,1:T(8,128)S(1)} fusion(f32[64,16384]{1,0:T(8,128)} %bitcast.49, bf16[16384,128]{1,0:T(8,128)(2,1)} %get-tuple-element.9, s32[]{:T(128)} %bitcast.3, s32[16384]{0:T(1024)S(1)} %iota_add_fusion), kind=kOutput, calls=%fused_computation.69 | convolution fusion | flops 1625292800 | bytes 8486916 | tf_op jit(solution)/shard_map/dot_general | solution.py:34
  477.8 55.1 %psum.85 = f32[64,128]{0,1:T(8,128)S(1)} all-reduce(f32[64,128]{0,1:T(8,128)S(1)} %fusion.56), channel_id=1, replica_groups=mesh['row'=16,'col'=8] {'row'}, use_global_device_ids=true, to_apply=%region_1.2 | all-reduce | flops 8192 | bytes 65536 | tf_op jit(solution)/shard_map/psum | solution.py:37
  532.8 18.0 %all-reduce.5.cloned.1.call-done = (bf16[128,128]{1,0:T(8,128)(2,1)}, bf16[128,128]{1,0:T(8,128)(2,1)}, bf16[128,128]{1,0:T(8,128)(2,1)}, bf16[128,128]{1,0:T(8,128)(2,1)}) async-done(((bf16[128,128]{1,0:T(8,128)(2,1)}, bf16[128,128]{1,0:T(8,128)(2,1)}, bf16[128,128]{1,0:T(8,128)(2,1)}, bf16[128,128]{1,0:T(8,128)(2,1)}), (bf16[128,128]{1,0:T(8,128)(2,1)}, bf16[128,128]{1,0:T(8,128)(2,1)}, ...) | async-done | bytes 131088 | tf_op jit(solution)/shard_map/psum | solution.py:11
  550.8 1.0 fusion.83
  551.8 0.0 copy-start.7
  551.8 13.2 %convolution_subtract_fusion.3 = f32[64,16384]{1,0:T(8,128)S(1)} fusion(f32[64,16384]{1,0:T(8,128)} %bitcast.50, f32[64,128]{1,0:T(8,128)S(1)} %fusion.83, bf16[16384,128]{1,0:T(8,128)(2,1)} %get-tuple-element.9, s32[]{:T(128)} %bitcast.3, s32[16384]{0:T(1024)S(1)} %iota_add_fusion), kind=kOutput, calls=%fused_computation.3 | convolution fusion | flops 1626341376 | bytes 12681220 | tf_op jit(solution)/shard_map/dot_general | solution.py:44
  565.0 0.0 copy-start.9
  565.0 2.0 copy-done.9
  567.0 0.0 copy-done.7
  567.0 0.0 copy-start.2
  567.0 7.5 fusion.13
  574.5 53.1 %psum.88 = f32[64,128]{1,0:T(8,128)S(1)} all-reduce(f32[64,128]{1,0:T(8,128)S(1)} %fusion.13), channel_id=1, replica_groups=mesh['row'=16,'col'=8] {'row'}, use_global_device_ids=true, to_apply=%region_4.5 | all-reduce | flops 8192 | bytes 65536 | tf_op jit(solution)/shard_map/psum | solution.py:37
  627.7 0.0 copy-done.2
  627.7 0.2 fusion.84
  627.9 0.0 copy-start.6
  627.9 13.2 %convolution_subtract_fusion.2 = f32[64,16384]{1,0:T(8,128)S(1)} fusion(f32[64,16384]{1,0:T(8,128)} %copy-done.9, f32[64,128]{1,0:T(8,128)S(1)} %fusion.84, bf16[16384,128]{1,0:T(8,128)(2,1)} %get-tuple-element.10, s32[]{:T(128)} %bitcast.8, s32[16384]{0:T(1024)S(1)} %iota_add_fusion), kind=kOutput, calls=%fused_computation.2 | convolution fusion | flops 1626341376 | bytes 12681220 | tf_op jit(solution)/shard_map/dot_general | solution.py:44
  641.1 0.0 copy-start.10
  641.1 2.0 copy-done.10
  643.1 0.0 copy-done.6
  643.1 0.0 copy-start.1
  643.1 7.6 fusion.14
  650.7 53.2 %psum.91 = f32[64,128]{1,0:T(8,128)S(1)} all-reduce(f32[64,128]{1,0:T(8,128)S(1)} %fusion.14), channel_id=1, replica_groups=mesh['row'=16,'col'=8] {'row'}, use_global_device_ids=true, to_apply=%region_7.8 | all-reduce | flops 8192 | bytes 65536 | tf_op jit(solution)/shard_map/psum | solution.py:37
  703.9 0.0 copy-done.1
  703.9 0.2 fusion.85
  704.1 0.0 copy-start.5
  704.1 13.3 %convolution_subtract_fusion.1 = f32[64,16384]{1,0:T(8,128)S(1)} fusion(f32[64,16384]{1,0:T(8,128)} %copy-done.10, f32[64,128]{1,0:T(8,128)S(1)} %fusion.85, bf16[16384,128]{1,0:T(8,128)(2,1)} %get-tuple-element.11, s32[]{:T(128)} %bitcast.12, s32[16384]{0:T(1024)S(1)} %iota_add_fusion), kind=kOutput, calls=%fused_computation.1 | convolution fusion | flops 1626341376 | bytes 12681220 | tf_op jit(solution)/shard_map/dot_general | solution.py:44
  717.4 0.0 copy-start.8
  717.4 2.0 copy-done.8
  719.4 0.0 copy-done.5
  719.4 0.0 copy-start
  719.4 7.6 fusion.15
  727.0 52.9 %psum.94 = f32[64,128]{1,0:T(8,128)S(1)} all-reduce(f32[64,128]{1,0:T(8,128)S(1)} %fusion.15), channel_id=1, replica_groups=mesh['row'=16,'col'=8] {'row'}, use_global_device_ids=true, to_apply=%region_10.11 | all-reduce | flops 8192 | bytes 65536 | tf_op jit(solution)/shard_map/psum | solution.py:37
  779.9 0.0 copy-done
  779.9 0.2 fusion.86
  780.1 14.0 %convolution_subtract_fusion = f32[64,16384]{1,0:T(8,128)} fusion(f32[64,16384]{1,0:T(8,128)} %copy-done.8, f32[64,128]{1,0:T(8,128)S(1)} %fusion.86, bf16[16384,128]{1,0:T(8,128)(2,1)} %get-tuple-element.12, s32[]{:T(128)} %bitcast.16, s32[16384]{0:T(1024)S(1)} %iota_add_fusion), kind=kOutput, calls=%fused_computation | convolution fusion | flops 1626341376 | bytes 12681220 | tf_op jit(solution)/shard_map/dot_general | solution.py:44
  (1 shorter events, 0.0 us)
Async XLA Ops:
  6.5 454.8 %all-reduce.7.cloned.1.call-start = ((), (), s32[]{:S(2)}) async-start(), calls=%async_computation.3 | async-start | bytes 33554432 | tf_op jit(solution)/shard_map/psum | solution.py:11
  244.8 4.8 copy-start.3
  244.8 5.5 copy-start.4
  244.8 105.8 %all-to-all-start.1 = ((f32[8,64,2048]{2,1,0:T(8,128)}), f32[8,64,2048]{2,1,0:T(8,128)}, u32[]{:S(2)}, u32[]{:S(2)}) async-start(f32[8,64,2048]{2,1,0:T(8,128)} %all_to_all.29), calls=%async_computation.1 | async-start | bytes 8388608 | tf_op jit(solution)/shard_map/all_to_all | solution.py:25
  249.5 301.3 %all-reduce.5.cloned.1.call-start = ((), (), s32[]{:S(2)}) async-start(), calls=%async_computation.2 | async-start | bytes 262144 | tf_op jit(solution)/shard_map/psum | solution.py:11
  551.8 15.2 %copy-start.7 = (bf16[16384,128]{1,0:T(8,128)(2,1)S(1)}, bf16[16384,128]{1,0:T(8,128)(2,1)}, u32[]{:S(2)}) copy-start(bf16[16384,128]{1,0:T(8,128)(2,1)} %get-tuple-element.10) | copy-start | bytes 12582916
  565.0 2.0 copy-start.9
  567.0 60.7 %copy-start.2 = (bf16[128,128]{1,0:T(8,128)(2,1)S(1)}, bf16[128,128]{1,0:T(8,128)(2,1)}, u32[]{:S(2)}) copy-start(bf16[128,128]{1,0:T(8,128)(2,1)} %get-tuple-element.6) | copy-start | bytes 98308
  627.9 15.2 %copy-start.6 = (bf16[16384,128]{1,0:T(8,128)(2,1)S(1)}, bf16[16384,128]{1,0:T(8,128)(2,1)}, u32[]{:S(2)}) copy-start(bf16[16384,128]{1,0:T(8,128)(2,1)} %get-tuple-element.11) | copy-start | bytes 12582916
  641.1 2.0 copy-start.10
  643.1 60.8 %copy-start.1 = (bf16[128,128]{1,0:T(8,128)(2,1)S(1)}, bf16[128,128]{1,0:T(8,128)(2,1)}, u32[]{:S(2)}) copy-start(bf16[128,128]{1,0:T(8,128)(2,1)} %get-tuple-element.7) | copy-start | bytes 98308
  704.1 15.3 %copy-start.5 = (bf16[16384,128]{1,0:T(8,128)(2,1)S(1)}, bf16[16384,128]{1,0:T(8,128)(2,1)}, u32[]{:S(2)}) copy-start(bf16[16384,128]{1,0:T(8,128)(2,1)} %get-tuple-element.12) | copy-start | bytes 12582916
  717.4 2.0 copy-start.8
  719.4 60.6 %copy-start = (bf16[128,128]{1,0:T(8,128)(2,1)S(1)}, bf16[128,128]{1,0:T(8,128)(2,1)}, u32[]{:S(2)}) copy-start(bf16[128,128]{1,0:T(8,128)(2,1)} %get-tuple-element.8) | copy-start | bytes 98308
Sparse Core Ops, SparseCore 0:
  18.1 443.1 all-reduce.6
  464.0 86.7 all-reduce.4
where the time goes:
time: 812 us; the launch traced here: 801 us
  blocking collectives  436 us (54%)
  waiting for transfers between devices  224 us (28%)
  matrix products  94.4 us (12%)
  local copies, waits for them, and re-layouts  18.1 us (2%)
  between operations  16.5 us (2%)
    all_to_all x1, blocking collectives, local(): lax.all_to_all(eigvecs, ('row', 'col'), split_axis=1, concat_axis=0, tile...  222 us
    psum x4, blocking collectives, local(): projection = lax.psum(partial_sum, 'row')  214 us
    psum x2, waiting for transfers between devices, from_root(): return lax.psum(jnp.where(mine, value, jnp.zeros_like(value)), axis)  124 us
    all_to_all x1, waiting for transfers between devices, local(): lax.all_to_all(spread, 'col', split_axis=0, concat_axis=1, tiled=True)  99.6 us
    dot_general x4, matrix products, local(): jnp.dot(coeffs, reflector.T, precision=highest, preferred_element_type=jn...  53.6 us
    dot_general x4, matrix products, local(): jnp.dot(field, reflector, precision=highest, preferred_element_type=jnp.f...  39.2 us
  transfers between devices with their start and end apart: 3, of which 3 were waited for; matrix products, arithmetic and copies ran while one was open for 3% of the time, Pallas kernels for 0%

commit v1 on v0

--- a/solution.py
+++ b/solution.py
@@ -34,7 +34,8 @@
         partial_sum = jnp.dot(
             field, reflector, precision=highest, preferred_element_type=jnp.float32
         )
-        projection = lax.psum(partial_sum, "row")
+        pieces = lax.all_gather(partial_sum, "row")
+        projection = jnp.sum(pieces, axis=0)
         coeffs = jnp.dot(
             projection,
             triangle.astype(jnp.float32).T,

time: 812 us -> 703 us (0.87)
  blocking collectives: 436 us -> 299 us
  waiting for transfers between devices: 224 us -> 264 us
    psum x4 -> x0, blocking collectives: 214 us -> none  [local(): projection = lax.psum(partial_sum, 'row')]
    all_gather x0 -> x4, blocking collectives: none -> 77.4 us  [local(): pieces = lax.all_gather(partial_sum, 'row')]
    psum x2, waiting for transfers between devices: 124 us -> 165 us  [from_root(): return lax.psum(jnp.where(mine, value, jnp.zeros_like(value)), axis)]
  transfers between devices with their start and end apart: 3 -> 3, of which waited for: 3 -> 3; matrix products, arithmetic and copies ran while one was open for 3% -> 2% of each run, Pallas kernels for 0% -> 0%
where the time goes in v1:
time: 703 us; the launch traced here: 694 us
  blocking collectives  299 us (43%)
  waiting for transfers between devices  264 us (38%)
  matrix products  88.9 us (13%)
  between operations  16.4 us (2%)
  local copies, waits for them, and re-layouts  12.1 us (2%)
  other arithmetic  8.23 us (1%)
    all_to_all x1, blocking collectives, local(): lax.all_to_all(eigvecs, ('row', 'col'), split_axis=1, concat_axis=0, tile...  222 us
    psum x2, waiting for transfers between devices, from_root(): return lax.psum(jnp.where(mine, value, jnp.zeros_like(value)), axis)  165 us
    all_to_all x1, waiting for transfers between devices, local(): lax.all_to_all(spread, 'col', split_axis=0, concat_axis=1, tiled=True)  99.6 us
    all_gather x4, blocking collectives, local(): pieces = lax.all_gather(partial_sum, 'row')  77.4 us
    dot_general x4, matrix products, local(): jnp.dot(coeffs, reflector.T, precision=highest, preferred_element_type=jn...  53.6 us
    dot_general x4, matrix products, local(): jnp.dot(field, reflector, precision=highest, preferred_element_type=jnp.f...  33.7 us
  transfers between devices with their start and end apart: 3, of which 3 were waited for; matrix products, arithmetic and copies ran while one was open for 2% of the time, Pallas kernels for 0%

profile of v1, /device:TPU:0, one launch (start us, length us, event | category | flops | bytes accessed | tf_op | source)
XLA Modules:
  0.0 693.7 jit_solution(15025204466043644712)
XLA Ops:
  6.5 0.0 all-reduce.7.cloned.1.call-start
  6.5 1.5 fusion.82
  10.5 7.4 %select_bitcast_fusion = (bf16[16384,128]{1,0:T(8,128)(2,1)}, bf16[16384,128]{1,0:T(8,128)(2,1)}, bf16[16384,128]{1,0:T(8,128)(2,1)}, bf16[16384,128]{1,0:T(8,128)(2,1)}) fusion(bf16[1,16384,128]{2,1,0:T(8,128)(2,1)} %param.6, pred[]{:T(512)S(6)} %eq.34, pred[]{:T(512)S(6)} %eq.30, pred[]{:T(512)S(6)} %eq.28, pred[]{:T(512)S(6)} %eq.32), kind=kLoop, calls=%fused_computation.25 | loop fusion | flops 8388608 | bytes 20971524 | tf_op jit(solution)/shard_map/jit(_where)/select_n | solution.py:11
  18.0 0.0 all-reduce.7.cloned.1.call-update
  18.0 221.5 %all_to_all.35 = f32[4,128,2048]{2,0,1:T(4,128)} all-to-all(f32[4,128,2048]{2,0,1:T(4,128)} %bitcast.52), channel_id=1, replica_groups=mesh['row'=16,'col'=8] {'row','col'}, dimensions={1} | all-to-all | bytes 8388608 | tf_op jit(solution)/shard_map/all_to_all | solution.py:24
  239.5 5.3 all_to_all.29
  244.8 0.0 copy-start.3
  244.8 0.0 copy-start.4
  244.8 4.7 all-to-all-start.1
  249.5 0.0 all-reduce.5.cloned.1.call-start
  249.6 0.0 copy-done.3
  249.6 0.7 select_bitcast_fusion.4
  250.2 0.0 all-reduce.5.cloned.1.call-update
  250.3 0.0 copy-done.4
  250.3 0.7 fusion.81
  251.0 99.6 %all-to-all-done.1 = f32[8,64,2048]{2,1,0:T(8,128)} async-done(((f32[8,64,2048]{2,1,0:T(8,128)}), f32[8,64,2048]{2,1,0:T(8,128)}, u32[]{:S(2)}, u32[]{:S(2)}) %all-to-all-start.1) | async-done | bytes 4194336 | tf_op jit(solution)/shard_map/all_to_all | solution.py:25
  350.6 4.7 copy.8
  355.3 106.0 %all-reduce.7.cloned.1.call-done = (bf16[16384,128]{1,0:T(8,128)(2,1)}, bf16[16384,128]{1,0:T(8,128)(2,1)}, bf16[16384,128]{1,0:T(8,128)(2,1)}, bf16[16384,128]{1,0:T(8,128)(2,1)}) async-done(((bf16[16384,128]{1,0:T(8,128)(2,1)}, bf16[16384,128]{1,0:T(8,128)(2,1)}, bf16[16384,128]{1,0:T(8,128)(2,1)}, bf16[16384,128]{1,0:T(8,128)(2,1)}), (bf16[16384,128]{1,0:T(8,128)(2,1)}, bf16[16384,128]{1,0:T(8,128)(2,1)}, ...) | async-done | bytes 16777232 | tf_op jit(solution)/shard_map/psum | solution.py:11
  461.3 10.8 %fusion.56 = f32[64,128]{1,0:T(8,128)S(1)} fusion(f32[64,16384]{1,0:T(8,128)} %bitcast.53, bf16[16384,128]{1,0:T(8,128)(2,1)} %get-tuple-element.9, s32[]{:T(128)} %bitcast.3, s32[16384]{0:T(1024)S(1)} %iota_add_fusion), kind=kOutput, calls=%fused_computation.69 | convolution fusion | flops 1625292800 | bytes 8486916 | tf_op jit(solution)/shard_map/dot_general | solution.py:34
  472.2 20.0 %all-gather = f32[1024,128]{1,0:T(8,128)S(1)} all-gather(f32[64,128]{1,0:T(8,128)S(1)} %fusion.56), channel_id=2, replica_groups=mesh['row'=16,'col'=8] {'row'}, dimensions={0}, use_global_device_ids=true | all-gather | bytes 557056 | tf_op jit(solution)/shard_map/all_gather | solution.py:37
  492.1 58.7 %all-reduce.5.cloned.1.call-done = (bf16[128,128]{1,0:T(8,128)(2,1)}, bf16[128,128]{1,0:T(8,128)(2,1)}, bf16[128,128]{1,0:T(8,128)(2,1)}, bf16[128,128]{1,0:T(8,128)(2,1)}) async-done(((bf16[128,128]{1,0:T(8,128)(2,1)}, bf16[128,128]{1,0:T(8,128)(2,1)}, bf16[128,128]{1,0:T(8,128)(2,1)}, bf16[128,128]{1,0:T(8,128)(2,1)}), (bf16[128,128]{1,0:T(8,128)(2,1)}, bf16[128,128]{1,0:T(8,128)(2,1)}, ...) | async-done | bytes 131088 | tf_op jit(solution)/shard_map/psum | solution.py:11
  550.8 0.9 fusion.83
  551.8 0.0 copy-start.7
  551.8 13.2 %convolution_subtract_fusion.3 = f32[64,16384]{1,0:T(8,128)S(1)} fusion(f32[64,16384]{1,0:T(8,128)} %bitcast.54, f32[64,128]{1,0:T(8,128)S(1)} %fusion.83, bf16[16384,128]{1,0:T(8,128)(2,1)} %get-tuple-element.9, s32[]{:T(128)} %bitcast.3, s32[16384]{0:T(1024)S(1)} %iota_add_fusion), kind=kOutput, calls=%fused_computation.3 | convolution fusion | flops 1626341376 | bytes 12681220 | tf_op jit(solution)/shard_map/dot_general | solution.py:45
  565.0 0.0 copy-start.9
  565.0 0.0 copy-done.7
  565.0 0.0 copy-start.2
  565.0 7.6 %fusion.13 = f32[64,128]{1,0:T(8,128)S(1)} fusion(f32[64,16384]{1,0:T(8,128)S(1)} %convolution_subtract_fusion.3, bf16[16384,128]{1,0:T(8,128)(2,1)S(1)} %copy-done.7, s32[]{:T(128)} %bitcast.9, s32[16384]{0:T(1024)S(1)} %iota_add_fusion), kind=kOutput, calls=%fused_computation.22 | convolution fusion | flops 1625292800 | bytes 8486916 | tf_op jit(solution)/shard_map/dot_general | solution.py:34
  572.6 0.0 copy-done.9
  572.6 20.5 %all-gather.1 = f32[1024,128]{1,0:T(8,128)S(1)} all-gather(f32[64,128]{1,0:T(8,128)S(1)} %fusion.13), channel_id=3, replica_groups=mesh['row'=16,'col'=8] {'row'}, dimensions={0}, use_global_device_ids=true | all-gather | bytes 557056 | tf_op jit(solution)/shard_map/all_gather | solution.py:37
  593.1 0.0 copy-done.2
  593.1 0.2 fusion.84
  593.3 0.0 copy-start.6
  593.3 13.2 %convolution_subtract_fusion.2 = f32[64,16384]{1,0:T(8,128)S(1)} fusion(f32[64,16384]{1,0:T(8,128)} %copy-done.9, f32[64,128]{1,0:T(8,128)S(1)} %fusion.84, bf16[16384,128]{1,0:T(8,128)(2,1)} %get-tuple-element.10, s32[]{:T(128)} %bitcast.9, s32[16384]{0:T(1024)S(1)} %iota_add_fusion), kind=kOutput, calls=%fused_computation.2 | convolution fusion | flops 1626341376 | bytes 12681220 | tf_op jit(solution)/shard_map/dot_general | solution.py:45
  606.5 0.0 copy-start.10
  606.5 0.0 copy-done.6
  606.5 0.0 copy-start.1
  606.5 7.6 %fusion.14 = f32[64,128]{1,0:T(8,128)S(1)} fusion(f32[64,16384]{1,0:T(8,128)S(1)} %convolution_subtract_fusion.2, bf16[16384,128]{1,0:T(8,128)(2,1)S(1)} %copy-done.6, s32[]{:T(128)} %bitcast.14, s32[16384]{0:T(1024)S(1)} %iota_add_fusion), kind=kOutput, calls=%fused_computation.23 | convolution fusion | flops 1625292800 | bytes 8486916 | tf_op jit(solution)/shard_map/dot_general | solution.py:34
  614.2 0.0 copy-done.10
  614.2 17.9 %all-gather.2 = f32[1024,128]{1,0:T(8,128)S(1)} all-gather(f32[64,128]{1,0:T(8,128)S(1)} %fusion.14), channel_id=4, replica_groups=mesh['row'=16,'col'=8] {'row'}, dimensions={0}, use_global_device_ids=true | all-gather | bytes 557056 | tf_op jit(solution)/shard_map/all_gather | solution.py:37
  632.1 0.0 copy-done.1
  632.2 0.2 fusion.85
  632.4 0.0 copy-start.5
  632.4 13.3 %convolution_subtract_fusion.1 = f32[64,16384]{1,0:T(8,128)S(1)} fusion(f32[64,16384]{1,0:T(8,128)} %copy-done.10, f32[64,128]{1,0:T(8,128)S(1)} %fusion.85, bf16[16384,128]{1,0:T(8,128)(2,1)} %get-tuple-element.11, s32[]{:T(128)} %bitcast.14, s32[16384]{0:T(1024)S(1)} %iota_add_fusion), kind=kOutput, calls=%fused_computation.1 | convolution fusion | flops 1626341376 | bytes 12681220 | tf_op jit(solution)/shard_map/dot_general | solution.py:45
  645.7 0.0 copy-start.8
  645.7 0.0 copy-done.5
  645.7 0.0 copy-start
  645.7 7.7 %fusion.15 = f32[64,128]{1,0:T(8,128)S(1)} fusion(f32[64,16384]{1,0:T(8,128)S(1)} %convolution_subtract_fusion.1, bf16[16384,128]{1,0:T(8,128)(2,1)S(1)} %copy-done.5, s32[]{:T(128)} %bitcast.19, s32[16384]{0:T(1024)S(1)} %iota_add_fusion), kind=kOutput, calls=%fused_computation.24 | convolution fusion | flops 1625292800 | bytes 8486916 | tf_op jit(solution)/shard_map/dot_general | solution.py:34
  653.4 0.0 copy-done.8
  653.4 19.0 %all-gather.3 = f32[1024,128]{1,0:T(8,128)S(1)} all-gather(f32[64,128]{1,0:T(8,128)S(1)} %fusion.15), channel_id=5, replica_groups=mesh['row'=16,'col'=8] {'row'}, dimensions={0}, use_global_device_ids=true | all-gather | bytes 557056 | tf_op jit(solution)/shard_map/all_gather | solution.py:37
  672.5 0.0 copy-done
  672.5 0.2 fusion.86
  672.7 14.0 %convolution_subtract_fusion = f32[64,16384]{1,0:T(8,128)} fusion(f32[64,16384]{1,0:T(8,128)} %copy-done.8, f32[64,128]{1,0:T(8,128)S(1)} %fusion.86, bf16[16384,128]{1,0:T(8,128)(2,1)} %get-tuple-element.12, s32[]{:T(128)} %bitcast.19, s32[16384]{0:T(1024)S(1)} %iota_add_fusion), kind=kOutput, calls=%fused_computation | convolution fusion | flops 1626341376 | bytes 12681220 | tf_op jit(solution)/shard_map/dot_general | solution.py:45
  (5 shorter events, 0.1 us)
Async XLA Ops:
  6.5 454.8 %all-reduce.7.cloned.1.call-start = ((), (), s32[]{:S(2)}) async-start(), calls=%async_computation.3 | async-start | bytes 33554432 | tf_op jit(solution)/shard_map/psum | solution.py:11
  244.8 4.8 copy-start.3
  244.8 5.5 copy-start.4
  244.8 105.8 %all-to-all-start.1 = ((f32[8,64,2048]{2,1,0:T(8,128)}), f32[8,64,2048]{2,1,0:T(8,128)}, u32[]{:S(2)}, u32[]{:S(2)}) async-start(f32[8,64,2048]{2,1,0:T(8,128)} %all_to_all.29), calls=%async_computation.1 | async-start | bytes 8388608 | tf_op jit(solution)/shard_map/all_to_all | solution.py:25
  249.5 301.3 %all-reduce.5.cloned.1.call-start = ((), (), s32[]{:S(2)}) async-start(), calls=%async_computation.2 | async-start | bytes 262144 | tf_op jit(solution)/shard_map/psum | solution.py:11
  551.8 13.2 %copy-start.7 = (bf16[16384,128]{1,0:T(8,128)(2,1)S(1)}, bf16[16384,128]{1,0:T(8,128)(2,1)}, u32[]{:S(2)}) copy-start(bf16[16384,128]{1,0:T(8,128)(2,1)} %get-tuple-element.10) | copy-start | bytes 12582916
  565.0 7.6 %copy-start.9 = (f32[64,16384]{1,0:T(8,128)}, f32[64,16384]{1,0:T(8,128)S(1)}, u32[]{:S(2)}) copy-start(f32[64,16384]{1,0:T(8,128)S(1)} %convolution_subtract_fusion.3) | copy-start | bytes 12582916
  565.0 28.1 %copy-start.2 = (bf16[128,128]{1,0:T(8,128)(2,1)S(1)}, bf16[128,128]{1,0:T(8,128)(2,1)}, u32[]{:S(2)}) copy-start(bf16[128,128]{1,0:T(8,128)(2,1)} %get-tuple-element.6) | copy-start | bytes 98308
  593.3 13.2 %copy-start.6 = (bf16[16384,128]{1,0:T(8,128)(2,1)S(1)}, bf16[16384,128]{1,0:T(8,128)(2,1)}, u32[]{:S(2)}) copy-start(bf16[16384,128]{1,0:T(8,128)(2,1)} %get-tuple-element.11) | copy-start | bytes 12582916
  606.5 7.7 %copy-start.10 = (f32[64,16384]{1,0:T(8,128)}, f32[64,16384]{1,0:T(8,128)S(1)}, u32[]{:S(2)}) copy-start(f32[64,16384]{1,0:T(8,128)S(1)} %convolution_subtract_fusion.2) | copy-start | bytes 12582916
  606.5 25.6 %copy-start.1 = (bf16[128,128]{1,0:T(8,128)(2,1)S(1)}, bf16[128,128]{1,0:T(8,128)(2,1)}, u32[]{:S(2)}) copy-start(bf16[128,128]{1,0:T(8,128)(2,1)} %get-tuple-element.7) | copy-start | bytes 98308
  632.4 13.3 %copy-start.5 = (bf16[16384,128]{1,0:T(8,128)(2,1)S(1)}, bf16[16384,128]{1,0:T(8,128)(2,1)}, u32[]{:S(2)}) copy-start(bf16[16384,128]{1,0:T(8,128)(2,1)} %get-tuple-element.12) | copy-start | bytes 12582916
  645.7 7.7 %copy-start.8 = (f32[64,16384]{1,0:T(8,128)}, f32[64,16384]{1,0:T(8,128)S(1)}, u32[]{:S(2)}) copy-start(f32[64,16384]{1,0:T(8,128)S(1)} %convolution_subtract_fusion.1) | copy-start | bytes 12582916
  645.7 26.8 %copy-start = (bf16[128,128]{1,0:T(8,128)(2,1)S(1)}, bf16[128,128]{1,0:T(8,128)(2,1)}, u32[]{:S(2)}) copy-start(bf16[128,128]{1,0:T(8,128)(2,1)} %get-tuple-element.8) | copy-start | bytes 98308
Sparse Core Ops, SparseCore 0:
  18.1 443.1 all-reduce.6
  464.0 86.7 all-reduce.4
